TPU v7x, 32 devices: a whole 2x2x4 slice. The times are simulated.
32 devices in a mesh: groups: 2 (over y), gx: 16 (over z, x, core).
Axes of the slice: x: 2, y: 2, z: 4, core: 2. Of those that a mesh axis runs over, the one named last changes fastest.
Arguments:
- grad_out: bfloat16 [64, 4, 128, 128], P(('groups', 'gx')), parts along dimension 0, may hold values from -6 to 6
- inputs: bfloat16 [64, 4, 128, 128], P(('groups', 'gx')), parts along dimension 0, may hold values from -6 to 6
- pre_first: bfloat16 [64, 4, 128, 128], P(('groups', 'gx')), parts along dimension 0, may hold values from -6 to 6
- pre_second: bfloat16 [64, 4, 128, 128], P(('groups', 'gx')), parts along dimension 0, may hold values from -6 to 6
- filter_first: bfloat16 [3456, 128], P('gx'), may hold values from -0.109375 to 0.109375
- filter_second: bfloat16 [3456, 128], P('gx'), may hold values from -0.109375 to 0.109375
Outputs:
- grad_inputs: bfloat16 [64, 4, 128, 128], P(('groups', 'gx')), parts along dimension 0
- grad_filter_first: float32 [3456, 256], P('gx', 'groups'), parts along dimension 1
- grad_filter_second: float32 [3456, 256], P('gx', 'groups'), parts along dimension 1
There are 2 independent parts, one for each index of `groups`. A program takes and returns all parts, laid end to end along the dimension named above; an argument that names none is the same for every part. Nothing has to cross between parts.
All inputs are finite; a program needn't handle non-finite values.
Results may differ from a plain program's by a relative error of at most 0.0058.
Values may be sent and summed in bfloat16 or wider, within the bound.
A program may use at most 64 MiB of HBM per device.

v0:
```python
import functools
import math

import jax
import jax.numpy as jnp
from jax import lax
from jax.experimental import pallas as pl
from jax.experimental.pallas import tpu as pltpu
from jax.sharding import PartitionSpec as P

inv_root_two = 0.7071067811865476
inv_root_twopi = 0.3989422804014327
tap_shifts = ((-1, -1), (-1, 0), (-1, 1), (0, -1), (0, 0), (0, 1), (1, -1), (1, 0), (1, 1))


def with_halo(block, sides, width):
    for axis, dim in sides:
        count = lax.axis_size(axis)
        forward = [(i, i + 1) for i in range(count - 1)]
        backward = [(target, source) for source, target in forward]
        low = lax.ppermute(
            lax.slice_in_dim(block, block.shape[dim] - width, None, axis=dim), axis, forward
        )
        high = lax.ppermute(lax.slice_in_dim(block, 0, width, axis=dim), axis, backward)
        block = jnp.concatenate([low, block, high], axis=dim)
    return block


def gelu_parts(value):
    normal_cdf = 0.5 * (1.0 + lax.erf(value * inv_root_two))
    return (value * normal_cdf, normal_cdf + value * jnp.exp(-0.5 * value * value) * inv_root_twopi)


def pad_sides(extended):
    return jnp.pad(extended, ((0, 0), (1, 1), (1, 1), (0, 0)))


def stack_taps(padded, direction, z_cells):
    return jnp.concatenate(
        [
            padded[:, :, 1 + direction * shift_z : 1 + direction * shift_z + z_cells]
            for shift_z in (-1, 0, 1)
        ],
        axis=3,
    )


def window(stacked, direction, shift_x, shift_y, x_cells, y_cells):
    start_x = 1 + direction * shift_x
    start_y = 1 + direction * shift_y
    return stacked[start_x : start_x + x_cells, start_y : start_y + y_cells]


def back_data(stacked, full_filter, shape):
    x_cells, y_cells, z_cells, channels = shape
    kernel = full_filter.reshape(3, 3, 3, channels, channels)
    running = jnp.zeros((x_cells * y_cells * z_cells, channels), jnp.float32)
    for shift_x, shift_y in tap_shifts:
        tap_matrix = jnp.transpose(kernel[shift_x + 1, shift_y + 1], (0, 2, 1)).reshape(
            3 * channels, channels
        )
        piece = window(stacked, -1, shift_x, shift_y, x_cells, y_cells).reshape(-1, 3 * channels)
        running = running + jnp.dot(piece, tap_matrix, preferred_element_type=jnp.float32)
    return running.reshape(shape)


def filter_from_inputs(stacked, grads, shape):
    x_cells, y_cells, z_cells, channels = shape
    flat_grads = grads.reshape(-1, channels)
    blocks = []
    for shift_x, shift_y in tap_shifts:
        piece = window(stacked, 1, shift_x, shift_y, x_cells, y_cells).reshape(-1, 3 * channels)
        product = lax.dot_general(
            piece, flat_grads, (((0,), (0,)), ((), ())), preferred_element_type=jnp.float32
        )
        blocks.append(product.reshape(3, channels, channels))
    return jnp.stack(blocks).reshape(27 * channels, channels)


def on_device(grad_out, inputs, pre_first, pre_second, filter_first, filter_second):
    shape = grad_out.shape
    x_cells, y_cells, z_cells, channels = shape
    full_first, full_second = (
        lax.all_gather(filter_first, "gx", axis=0, tiled=True),
        lax.all_gather(filter_second, "gx", axis=0, tiled=True),
    )
    grad_scale = 1.0 / math.sqrt(x_cells * lax.axis_size("gx") * y_cells * z_cells)
    unused_value, slope_two = gelu_parts(pre_second.astype(jnp.float32))
    grad_two = (grad_out.astype(jnp.float32) * slope_two).astype(jnp.bfloat16)
    act_one, slope_one = gelu_parts(pre_first.astype(jnp.float32))
    act_one = act_one.astype(jnp.bfloat16)
    extended_two = pad_sides(with_halo(grad_two, (("gx", 0),), 1))
    stacked_two = stack_taps(extended_two, -1, z_cells)
    grad_act = back_data(stacked_two, full_second, shape)
    extended_act = pad_sides(with_halo(act_one, (("gx", 0),), 1))
    filt_two = filter_from_inputs(stack_taps(extended_act, 1, z_cells), grad_two, shape)
    owned_two = lax.psum_scatter(filt_two * grad_scale, "gx", scatter_dimension=0, tiled=True)
    grad_one = (grad_act * slope_one).astype(jnp.bfloat16)
    extended_one = pad_sides(with_halo(grad_one, (("gx", 0),), 1))
    stacked_one = stack_taps(extended_one, -1, z_cells)
    grad_in = back_data(stacked_one, full_first, shape).astype(jnp.bfloat16)
    extended_in = pad_sides(with_halo(inputs, (("gx", 0),), 1))
    filt_one = filter_from_inputs(stack_taps(extended_in, 1, z_cells), grad_one, shape)
    owned_one = lax.psum_scatter(filt_one * grad_scale, "gx", scatter_dimension=0, tiled=True)
    return (grad_in, owned_one, owned_two)


MESH = pl.DeviceIdType.MESH
sub = 8


def shift_z(block, shift):
    if shift == 0:
        return block
    cells = block.shape[0]
    row = lax.broadcasted_iota(jnp.int32, block.shape, 0)
    edge = 0 if shift > 0 else cells - 1
    return jnp.where(row == edge, 0.0, pltpu.roll(block, shift % cells, 0))


def kernel(
    n, go, xin, p1, p2, f1, f2, gin, own1, own2,
    fbuf, wbuf, gext, abuf, ahalo, sat, gcat, slope, part, s1, r1, s2, r2, s3, r3,
    halo_s, halo_r, agz_s, agz_r, agx_s, agx_r, agy_s, agy_r, agc_s, agc_r,
    rs1_s, rs1_r, rs2_s, rs2_r, rs3_s, rs3_r,
):
    xs, ys, zs, ch = go.shape
    units = f1.shape[0]
    hi = n // 4
    group, me = lax.axis_index("groups"), lax.axis_index("gx")
    core = me % 2
    mid = (me // 2) % 2
    top = me // 4
    partner = me + 1 - 2 * core
    across = me + 2 - 4 * mid

    def owner(t, m, c):
        return (t * 2 + m) * 2 + c

    def chunk(t, m, c):
        return pl.ds(owner(t, m, c) * units, units)

    def ahead(d):
        return lax.rem(top + d, hi)

    def behind(d):
        return lax.rem(top + hi - d, hi)

    lead = core == group
    sent = []

    def push(src, dst, send, recv, target, plane=group, keep=True):
        copy = pltpu.make_async_remote_copy(
            src_ref=src, dst_ref=dst, send_sem=send, recv_sem=recv,
            device_id=(plane, target), device_id_type=MESH,
        )
        copy.start()
        if keep:
            sent.append(copy)

    def arrive(dst, send, recv):
        pltpu.make_async_remote_copy(
            src_ref=dst, dst_ref=dst, send_sem=send, recv_sem=recv,
            device_id=(group, partner), device_id_type=MESH,
        ).wait_recv()

    barrier = pltpu.get_barrier_semaphore()
    peers = [partner, across, lax.rem(me + 1, n), lax.rem(me + n - 1, n)]
    peers += [owner(ahead(d), mid, core) for d in range(1, hi)]
    for peer in peers:
        pl.semaphore_signal(barrier, inc=1, device_id=(group, peer), device_id_type=MESH)
    pl.semaphore_signal(barrier, inc=1, device_id=(1 - group, me), device_id_type=MESH)
    pl.semaphore_wait(barrier, len(peers) + 1)

    filters = (f2, f1)

    def when_relay(f):
        return pl.when(lead) if f else lambda run: run()

    def gather_own(f):
        mine = fbuf.at[f, chunk(top, mid, core)]
        src = filters[f]
        push(src, mine, agc_s.at[f, 0], agc_r.at[f, 0], partner)

        @when_relay(f)
        def _():
            for d in range(1, hi):
                push(
                    src, mine, agz_s.at[f, d], agz_r.at[f, d],
                    owner(ahead(d), mid, core), keep=False,
                )
            push(src, mine, agx_s.at[f, 0], agx_r.at[f, 0], across, keep=False)

        fbuf[f, chunk(top, mid, core)] = src[...]

    def hand_on(f, got, k):
        if f:
            push(got, got, agy_s.at[f, k], agy_r.at[f, k], me, 1 - group, False)
        push(got, got, agc_s.at[f, k], agc_r.at[f, k], partner, keep=False)

    def gather_top(f):
        @when_relay(f)
        def _():
            for d in range(1, hi):
                got = fbuf.at[f, chunk(behind(d), mid, core)]
                arrive(got, agz_s.at[f, d], agz_r.at[f, d])
                push(got, got, agx_s.at[f, d], agx_r.at[f, d], across, keep=False)
                hand_on(f, got, d)

    def gather_mid(f):
        @when_relay(f)
        def _():
            for d in range(hi):
                got = fbuf.at[f, chunk(behind(d), 1 - mid, core)]
                arrive(got, agx_s.at[f, d], agx_r.at[f, d])
                hand_on(f, got, hi + d)

    def gather_follow(f):
        @pl.when(jnp.logical_not(lead))
        def _():
            for k in range(1, 2 * hi):
                which = mid if k < hi else 1 - mid
                got = fbuf.at[f, chunk(behind(k % hi), which, core)]
                arrive(got, agy_s.at[f, k], agy_r.at[f, k])
                push(got, got, agc_s.at[f, k], agc_r.at[f, k], partner, keep=False)

    def gather_core(f):
        for m in range(2):
            for d in range(hi):
                which = mid if m == 0 else 1 - mid
                got = fbuf.at[f, chunk(behind(d), which, 1 - core)]
                arrive(got, agc_s.at[f, m * hi + d], agc_r.at[f, m * hi + d])
        taps = 3 * ch // sub
        for ab in range(9):
            rows = fbuf[f, ab * taps : (ab + 1) * taps].astype(jnp.float32)
            wbuf[f, :, ab * ch : (ab + 1) * ch] = rows.reshape(3 * ch, ch).astype(jnp.bfloat16)

    def halo_copy(h, first, last, low, high):
        to_left = pltpu.make_async_remote_copy(
            src_ref=first, dst_ref=high, send_sem=halo_s.at[h, 0], recv_sem=halo_r.at[h, 1],
            device_id=(group, lax.rem(me + n - 1, n)), device_id_type=MESH,
        )
        to_right = pltpu.make_async_remote_copy(
            src_ref=last, dst_ref=low, send_sem=halo_s.at[h, 1], recv_sem=halo_r.at[h, 0],
            device_id=(group, lax.rem(me + 1, n)), device_id_type=MESH,
        )

        @pl.when(me > 0)
        def _():
            to_left.start()

        @pl.when(me < n - 1)
        def _():
            to_right.start()

        return to_left, to_right, low, high, h

    def halo_wait(halo):
        _, _, low, high, h = halo

        @pl.when(me > 0)
        def _():
            arrive(low, halo_s.at[h, 0], halo_r.at[h, 0])

        @pl.when(me == 0)
        def _():
            low[...] = jnp.zeros(low.shape, low.dtype)

        @pl.when(me < n - 1)
        def _():
            arrive(high, halo_s.at[h, 1], halo_r.at[h, 1])

        @pl.when(me == n - 1)
        def _():
            high[...] = jnp.zeros(high.shape, high.dtype)

    def grad_halo(h, f):
        inner = pl.ds(1, ys)
        return halo_copy(
            h, gext.at[f, 1, inner], gext.at[f, xs, inner],
            gext.at[f, 0, inner], gext.at[f, xs + 1, inner],
        )

    def saved_halo(h, s, block):
        return halo_copy(h, block.at[0], block.at[xs - 1], ahalo.at[s, 0], ahalo.at[s, 1])

    def keep_shifts(f, x, y, value):
        for c in (-1, 0, 1):
            gcat[f, x + 1, y + 1, :, (c + 1) * ch : (c + 2) * ch] = shift_z(value, c).astype(
                jnp.bfloat16
            )

    def keep_grad(f, x, y, value):
        gext[f, x + 1, y + 1] = value.astype(jnp.bfloat16)
        keep_shifts(f, x, y, value)

    def halo_shifts(f):
        for x in (-1, xs):
            for y in range(ys):
                keep_shifts(f, x, y, gext[f, x + 1, y + 1].astype(jnp.float32))

    def turn(s, layer, block):
        for y in range(ys):
            sat[s, layer, :, (y + 1) * zs : (y + 2) * zs] = block[y].T

    def filter_terms(s):
        for a in range(3):
            lhs = jnp.concatenate(
                [
                    jnp.concatenate(
                        [sat[s, x + a, :, b * zs : (b + ys) * zs] for x in range(xs)], axis=1
                    )
                    for b in range(3)
                ],
                axis=0,
            )
            rhs = gcat[s, 1 : xs + 1, 1 : ys + 1].reshape(xs * ys * zs, 3 * ch)
            out = jnp.dot(lhs, rhs, preferred_element_type=jnp.float32)
            per = ch // sub
            for b in range(3):
                for c in range(3):
                    at = (9 * a + 3 * b + c) * per
                    part[s, at : at + per] = out[
                        b * ch : (b + 1) * ch, c * ch : (c + 1) * ch
                    ].reshape(per, sub, ch)

    def filter_terms_halo(s):
        lhs = jnp.concatenate([sat[s, x + 1, :, zs : (ys + 1) * zs] for x in range(xs)], axis=1)
        per = ch // sub
        for a in (0, -1, 1):
            for b in (-1, 0, 1):
                rhs = gcat[s, 1 - a : 1 - a + xs, 1 - b : 1 - b + ys].reshape(
                    xs * ys * zs, 3 * ch
                )
                out = jnp.dot(lhs, rhs, preferred_element_type=jnp.float32)
                for c in range(3):
                    at = (9 * (a + 1) + 3 * (b + 1) + c) * per
                    part[s, at : at + per] = out[:, c * ch : (c + 1) * ch].reshape(per, sub, ch)

    def scatter_core(s):
        for m in range(2):
            which = 1 - mid if m == 0 else mid
            for t in range(hi):
                s1[s, m, t] = part[s, chunk(t, which, 1 - core)].astype(jnp.bfloat16)
            push(s1.at[s, m], r1.at[s, m], rs1_s.at[s, m], rs1_r.at[s, m], partner)

    def scatter_mid(s):
        arrive(r1.at[s, 0], rs1_s.at[s, 0], rs1_r.at[s, 0])
        for d in [*range(1, hi), 0]:
            t = ahead(d)
            s2[s, t] = (
                part[s, chunk(t, 1 - mid, core)] + r1[s, 0, t].astype(jnp.float32)
            ).astype(jnp.bfloat16)
            push(s2.at[s, t], r2.at[s, t], rs2_s.at[s, d], rs2_r.at[s, d], across)

    def total(s, t):
        return (
            part[s, chunk(t, mid, core)]
            + r1[s, 1, t].astype(jnp.float32)
            + r2[s, t].astype(jnp.float32)
        )

    def scatter_top(s):
        arrive(r1.at[s, 1], rs1_s.at[s, 1], rs1_r.at[s, 1])
        for d in range(1, hi):
            arrive(r2.at[s, ahead(d)], rs2_s.at[s, d], rs2_r.at[s, d])
            s3[s, d] = total(s, ahead(d)).astype(jnp.bfloat16)
            push(
                s3.at[s, d], r3.at[s, d], rs3_s.at[s, d], rs3_r.at[s, d],
                owner(ahead(d), mid, core),
            )

    def scatter_end(s, out):
        arrive(r2.at[s, top], rs2_s.at[s, 0], rs2_r.at[s, 0])
        value = total(s, top)
        for d in range(1, hi):
            arrive(r3.at[s, d], rs3_s.at[s, d], rs3_r.at[s, d])
            value = value + r3[s, d].astype(jnp.float32)
        out[...] = value

    def layer_back(f, x):
        lhs = jnp.concatenate(
            [
                gext[f, x + 1 - a, 1 - b : 1 - b + ys].reshape(ys * zs, ch)
                for a in (-1, 0, 1)
                for b in (-1, 0, 1)
            ],
            axis=1,
        )
        wide = lax.dot_general(
            lhs, wbuf[f], (((1,), (1,)), ((), ())), preferred_element_type=jnp.float32
        )
        rows = []
        for y in range(ys):
            block = wide[y * zs : (y + 1) * zs]
            rows.append(
                shift_z(block[:, :ch], -1) + block[:, ch : 2 * ch] + shift_z(block[:, 2 * ch :], 1)
            )
        return rows

    gather_own(0)
    halo_in = saved_halo(0, 0, xin)
    gather_own(1)

    for f in range(2):
        for x in range(xs + 2):
            for y in (0, ys + 1):
                gext[f, x, y] = jnp.zeros((zs, ch), jnp.bfloat16)
                gcat[f, x, y] = jnp.zeros((zs, 3 * ch), jnp.bfloat16)
                sat[f, x, :, y * zs : (y + 1) * zs] = jnp.zeros((ch, zs), jnp.bfloat16)

    @pl.loop(0, xs * ys)
    def _(i):
        x, y = i // ys, i % ys
        _, slope_two = gelu_parts(p2[x, y].astype(jnp.float32))
        keep_grad(0, x, y, go[x, y].astype(jnp.float32) * slope_two)
        act, slope_one = gelu_parts(p1[x, y].astype(jnp.float32))
        abuf[x, y] = act.astype(jnp.bfloat16)
        slope[x, y] = slope_one

    halo_two = grad_halo(1, 0)
    gather_top(0)
    for x in range(xs):
        turn(0, x + 1, abuf[x])
        turn(1, x + 1, xin[x])
    gather_mid(0)
    halo_wait(halo_two)
    halo_shifts(0)
    filter_terms_halo(0)
    scatter_core(0)
    gather_core(0)
    gather_top(1)
    scatter_mid(0)
    for x in range(xs):
        for y, value in enumerate(layer_back(0, x)):
            keep_grad(1, x, y, value * slope[x, y])
    halo_wait(halo_in)
    turn(1, 0, ahalo[0, 0])
    turn(1, xs + 1, ahalo[0, 1])
    filter_terms(1)
    scatter_core(1)
    scatter_mid(1)
    halo_one = grad_halo(2, 1)
    gather_mid(1)
    scatter_top(0)
    gather_follow(1)
    scatter_top(1)
    gather_core(1)
    halo_wait(halo_one)
    for x in range(xs):
        for y, value in enumerate(layer_back(1, x)):
            gin[x, y] = value
    scatter_end(0, own2)
    scatter_end(1, own1)
    for copy in sent:
        copy.wait_send()

    def left(f, send):
        pltpu.make_async_remote_copy(
            src_ref=filters[f], dst_ref=filters[f], send_sem=send, recv_sem=agc_r.at[f, 0],
            device_id=(group, partner), device_id_type=MESH,
        ).wait_send()

    for f in range(2):
        for k in range(1, 2 * hi):
            left(f, agc_s.at[f, k])

    for f in range(2):

        @when_relay(f)
        def _():
            for d in range(1, hi):
                left(f, agz_s.at[f, d])
            for d in range(hi):
                left(f, agx_s.at[f, d])
            if f:
                for k in range(1, 2 * hi):
                    left(f, agy_s.at[f, k])

    for halo in (halo_two, halo_in, halo_one):

        @pl.when(me > 0)
        def _():
            halo[0].wait_send()

        @pl.when(me < n - 1)
        def _():
            halo[1].wait_send()


def fused(grad_out, inputs, pre_first, pre_second, filter_first, filter_second):
    n = lax.axis_size("gx")
    xs, ys, zs, ch = grad_out.shape
    rows = filter_first.shape[0]
    if rows % sub or n % 4 or n < 8 or lax.axis_size("groups") != 2:
        return on_device(grad_out, inputs, pre_first, pre_second, filter_first, filter_second)
    units, hi, bf = rows // sub, n // 4, jnp.bfloat16
    dma = pltpu.SemaphoreType.DMA
    piece = (units, sub, ch)
    gin, own1, own2 = pl.pallas_call(
        functools.partial(kernel, n),
        out_shape=(
            jax.ShapeDtypeStruct(grad_out.shape, jnp.float32),
            jax.ShapeDtypeStruct(piece, jnp.float32),
            jax.ShapeDtypeStruct(piece, jnp.float32),
        ),
        in_specs=[pl.BlockSpec(memory_space=pltpu.VMEM)] * 6,
        out_specs=[pl.BlockSpec(memory_space=pltpu.VMEM)] * 3,
        scratch_shapes=[
            pltpu.VMEM((2, n * units, sub, ch), bf),
            pltpu.VMEM((2, 3 * ch, 9 * ch), bf),
            pltpu.VMEM((2, xs + 2, ys + 2, zs, ch), bf),
            pltpu.VMEM((xs, ys, zs, ch), bf),
            pltpu.VMEM((1, 2, ys, zs, ch), bf),
            pltpu.VMEM((2, xs + 2, ch, (ys + 2) * zs), bf),
            pltpu.VMEM((2, xs + 2, ys + 2, zs, 3 * ch), bf),
            pltpu.VMEM((xs, ys, zs, ch), jnp.float32),
            pltpu.VMEM((2, n * units, sub, ch), jnp.float32),
            pltpu.VMEM((2, 2, hi) + piece, bf),
            pltpu.VMEM((2, 2, hi) + piece, bf),
            pltpu.VMEM((2, hi) + piece, bf),
            pltpu.VMEM((2, hi) + piece, bf),
            pltpu.VMEM((2, hi) + piece, bf),
            pltpu.VMEM((2, hi) + piece, bf),
            dma((3, 2)), dma((3, 2)),
            dma((2, hi)), dma((2, hi)),
            dma((2, hi)), dma((2, hi)),
            dma((2, 2 * hi)), dma((2, 2 * hi)),
            dma((2, 2 * hi)), dma((2, 2 * hi)),
            dma((2, 2)), dma((2, 2)),
            dma((2, hi)), dma((2, hi)),
            dma((2, hi)), dma((2, hi)),
        ],
        compiler_params=pltpu.CompilerParams(collective_id=0, has_side_effects=True),
    )(
        grad_out, inputs, pre_first, pre_second,
        filter_first.reshape(piece), filter_second.reshape(piece),
    )
    scale = 1.0 / math.sqrt(xs * n * ys * zs)
    return gin.astype(bf), own1.reshape(rows, ch) * scale, own2.reshape(rows, ch) * scale


def solution(mesh):
    return jax.shard_map(
        fused,
        mesh=mesh,
        in_specs=(
            P(("groups", "gx"), None, None, None),
            P(("groups", "gx"), None, None, None),
            P(("groups", "gx"), None, None, None),
            P(("groups", "gx"), None, None, None),
            P("gx", None),
            P("gx", None),
        ),
        out_specs=(P(("groups", "gx"), None, None, None), P("gx", "groups"), P("gx", "groups")),
        check_vma=False,
    )
```

profile of v0, /device:TPU:0, one launch (start us, length us, event | category | flops | bytes accessed | tf_op | source)
XLA Modules:
  0.0 43.7 jit_solution(12780278445871304521)
XLA Ops:
  0.6 40.5 %shard_map.85 = (f32[2,4,128,128]{3,2,1,0:T(8,128)}, f32[27,8,128]{2,1,0:T(8,128)}, f32[27,8,128]{2,1,0:T(8,128)}) custom-call(bf16[2,4,128,128]{3,2,1,0:T(8,128)(2,1)} %go.1, bf16[2,4,128,128]{3,2,1,0:T(8,128)(2,1)} %xin.1, bf16[2,4,128,128]{3,2,1,0:T(8,128)(2,1)} %p1.1, bf16[2,4,128,128]{3,2,1,0:T(8,128)(2,1)} %p2.1, bf16[27,8,128]{2,1,0:T(8,128)(2,1)} %bitcast.6, ...), custom_call_target="tpu_custom_call" | custom-call | tf_op jit(solution)/shard_map/pallas_call | solution.py:500
  41.1 0.0 copy-start
  41.2 0.0 copy-start.1
  41.2 1.8 %convert_element_type.3 = bf16[2,4,128,128]{3,2,1,0:T(8,128)(2,1)} convert(f32[2,4,128,128]{3,2,1,0:T(8,128)} %get-tuple-element.6) | non-fusion elementwise | flops 131072 | bytes 786432 | tf_op jit(solution)/shard_map/convert_element_type | solution.py:540
  43.0 0.0 copy-done
  43.0 0.0 copy-done.1
  43.0 0.7 %multiply_bitcast_fusion = (f32[216,128]{1,0:T(8,128)}, f32[216,128]{1,0:T(8,128)}) fusion(f32[27,8,128]{2,1,0:T(8,128)S(1)} %copy-done.1, f32[27,8,128]{2,1,0:T(8,128)S(1)} %copy-done), kind=kLoop, calls=%fused_computation | loop fusion | flops 55296 | bytes 442368 | tf_op jit(solution)/shard_map/mul | solution.py:540
Async XLA Ops:
  41.1 1.8 %copy-start = (f32[27,8,128]{2,1,0:T(8,128)S(1)}, f32[27,8,128]{2,1,0:T(8,128)}, u32[]{:S(2)}) copy-start(f32[27,8,128]{2,1,0:T(8,128)} %get-tuple-element.7) | copy-start | bytes 331780
  41.2 1.8 %copy-start.1 = (f32[27,8,128]{2,1,0:T(8,128)S(1)}, f32[27,8,128]{2,1,0:T(8,128)}, u32[]{:S(2)}) copy-start(f32[27,8,128]{2,1,0:T(8,128)} %get-tuple-element.8) | copy-start | bytes 331780
where the time goes:
time: 43.9 us; the launch traced here: 43.7 us
  Pallas kernels  40.5 us (92%)
  other arithmetic  2.53 us (6%)
  between operations  0.66 us (2%)
    pallas_call x1, Pallas kernels, fused(): pl.pallas_call(functools.partial(kernel, n), out_shape=(jax.ShapeDtypeStr...  40.5 us
    convert_element_type x1, other arithmetic, fused(): gin.astype(bf)  1.83 us

commit v1 on v0

v1 whole, which is shorter than its diff:
```python
import functools
import math

import jax
import jax.numpy as jnp
from jax import lax
from jax.experimental import pallas as pl
from jax.experimental.pallas import tpu as pltpu
from jax.sharding import PartitionSpec as P

inv_root_two = 0.7071067811865476
inv_root_twopi = 0.3989422804014327
tap_shifts = ((-1, -1), (-1, 0), (-1, 1), (0, -1), (0, 0), (0, 1), (1, -1), (1, 0), (1, 1))


def with_halo(block, sides, width):
    for axis, dim in sides:
        count = lax.axis_size(axis)
        forward = [(i, i + 1) for i in range(count - 1)]
        backward = [(target, source) for source, target in forward]
        low = lax.ppermute(
            lax.slice_in_dim(block, block.shape[dim] - width, None, axis=dim), axis, forward
        )
        high = lax.ppermute(lax.slice_in_dim(block, 0, width, axis=dim), axis, backward)
        block = jnp.concatenate([low, block, high], axis=dim)
    return block


def gelu_parts(value):
    normal_cdf = 0.5 * (1.0 + lax.erf(value * inv_root_two))
    return (value * normal_cdf, normal_cdf + value * jnp.exp(-0.5 * value * value) * inv_root_twopi)


def pad_sides(extended):
    return jnp.pad(extended, ((0, 0), (1, 1), (1, 1), (0, 0)))


def stack_taps(padded, direction, z_cells):
    return jnp.concatenate(
        [
            padded[:, :, 1 + direction * shift_z : 1 + direction * shift_z + z_cells]
            for shift_z in (-1, 0, 1)
        ],
        axis=3,
    )


def window(stacked, direction, shift_x, shift_y, x_cells, y_cells):
    start_x = 1 + direction * shift_x
    start_y = 1 + direction * shift_y
    return stacked[start_x : start_x + x_cells, start_y : start_y + y_cells]


def back_data(stacked, full_filter, shape):
    x_cells, y_cells, z_cells, channels = shape
    kernel = full_filter.reshape(3, 3, 3, channels, channels)
    running = jnp.zeros((x_cells * y_cells * z_cells, channels), jnp.float32)
    for shift_x, shift_y in tap_shifts:
        tap_matrix = jnp.transpose(kernel[shift_x + 1, shift_y + 1], (0, 2, 1)).reshape(
            3 * channels, channels
        )
        piece = window(stacked, -1, shift_x, shift_y, x_cells, y_cells).reshape(-1, 3 * channels)
        running = running + jnp.dot(piece, tap_matrix, preferred_element_type=jnp.float32)
    return running.reshape(shape)


def filter_from_inputs(stacked, grads, shape):
    x_cells, y_cells, z_cells, channels = shape
    flat_grads = grads.reshape(-1, channels)
    blocks = []
    for shift_x, shift_y in tap_shifts:
        piece = window(stacked, 1, shift_x, shift_y, x_cells, y_cells).reshape(-1, 3 * channels)
        product = lax.dot_general(
            piece, flat_grads, (((0,), (0,)), ((), ())), preferred_element_type=jnp.float32
        )
        blocks.append(product.reshape(3, channels, channels))
    return jnp.stack(blocks).reshape(27 * channels, channels)


def on_device(grad_out, inputs, pre_first, pre_second, filter_first, filter_second):
    shape = grad_out.shape
    x_cells, y_cells, z_cells, channels = shape
    full_first, full_second = (
        lax.all_gather(filter_first, "gx", axis=0, tiled=True),
        lax.all_gather(filter_second, "gx", axis=0, tiled=True),
    )
    grad_scale = 1.0 / math.sqrt(x_cells * lax.axis_size("gx") * y_cells * z_cells)
    unused_value, slope_two = gelu_parts(pre_second.astype(jnp.float32))
    grad_two = (grad_out.astype(jnp.float32) * slope_two).astype(jnp.bfloat16)
    act_one, slope_one = gelu_parts(pre_first.astype(jnp.float32))
    act_one = act_one.astype(jnp.bfloat16)
    extended_two = pad_sides(with_halo(grad_two, (("gx", 0),), 1))
    stacked_two = stack_taps(extended_two, -1, z_cells)
    grad_act = back_data(stacked_two, full_second, shape)
    extended_act = pad_sides(with_halo(act_one, (("gx", 0),), 1))
    filt_two = filter_from_inputs(stack_taps(extended_act, 1, z_cells), grad_two, shape)
    owned_two = lax.psum_scatter(filt_two * grad_scale, "gx", scatter_dimension=0, tiled=True)
    grad_one = (grad_act * slope_one).astype(jnp.bfloat16)
    extended_one = pad_sides(with_halo(grad_one, (("gx", 0),), 1))
    stacked_one = stack_taps(extended_one, -1, z_cells)
    grad_in = back_data(stacked_one, full_first, shape).astype(jnp.bfloat16)
    extended_in = pad_sides(with_halo(inputs, (("gx", 0),), 1))
    filt_one = filter_from_inputs(stack_taps(extended_in, 1, z_cells), grad_one, shape)
    owned_one = lax.psum_scatter(filt_one * grad_scale, "gx", scatter_dimension=0, tiled=True)
    return (grad_in, owned_one, owned_two)


MESH = pl.DeviceIdType.MESH
sub = 8


def shift_z(block, shift):
    if shift == 0:
        return block
    cells = block.shape[0]
    row = lax.broadcasted_iota(jnp.int32, block.shape, 0)
    edge = 0 if shift > 0 else cells - 1
    return jnp.where(row == edge, 0.0, pltpu.roll(block, shift % cells, 0))


def kernel(
    n, go_in, xin_in, p1_in, p2_in, f1_in, f2_in, gin, own1, own2,
    go, xin, p1, p2,
    fbuf, wbuf, gext, abuf, sat, gcat, slope, part, s1, r1, s2, r2, s3, r3,
    load, halo_s, halo_r, agz_s, agz_r, agx_s, agx_r, agy_s, agy_r, agc_s, agc_r,
    rs1_s, rs1_r, rs2_s, rs2_r, rs3_s, rs3_r,
):
    xs, ys, zs, ch = go.shape
    units = f1_in.shape[0]
    hi = n // 4
    grad_scale = 1.0 / math.sqrt(xs * n * ys * zs)
    group, me = lax.axis_index("groups"), lax.axis_index("gx")
    core = me % 2
    mid = (me // 2) % 2
    top = me // 4
    partner = me + 1 - 2 * core
    across = me + 2 - 4 * mid
    lead = core == group
    follower = jnp.logical_not(lead)
    upper = top // ((hi + 1) // 2)
    room = top + upper * (hi - 1 - 2 * top)
    place = top + (1 - upper) * (hi - 1 - 2 * top)

    def owner(t, m, c):
        return (t * 2 + m) * 2 + c

    def chunk(t, m, c):
        return pl.ds(owner(t, m, c) * units, units)

    def at_least(value, bound):
        return 1 - 1 // (1 + value // bound)

    def near(k):
        both = at_least(2 * room, k)
        step = both * ((k + 1) // 2) + (1 - both) * (k - room)
        return top + (1 - 2 * upper) * (1 - 2 * both * ((k + 1) % 2)) * step

    def from_far(i):
        return (1 - upper) * (hi - 1 - i) + upper * i

    def far_peer(i):
        return from_far(i + at_least(i + 1, place + 1))

    def remote(src, dst, send, recv, target, plane):
        return pltpu.make_async_remote_copy(
            src_ref=src, dst_ref=dst, send_sem=send, recv_sem=recv,
            device_id=(plane, target), device_id_type=MESH,
        )

    def push(src, dst, send, recv, target, plane=group):
        remote(src, dst, send, recv, target, plane).start()

    def arrive(dst, recv):
        remote(dst, dst, halo_s.at[0, 0], recv, partner, group).wait_recv()

    barrier = pltpu.get_barrier_semaphore()
    peers = [partner, across, lax.rem(me + 1, n), lax.rem(me + n - 1, n)]
    peers += [owner(near(k), mid, core) for k in range(1, hi)]
    for peer in peers:
        pl.semaphore_signal(barrier, inc=1, device_id=(group, peer), device_id_type=MESH)
    pl.semaphore_signal(barrier, inc=1, device_id=(1 - group, me), device_id_type=MESH)

    own_chunk = chunk(top, mid, core)
    loads = [
        pltpu.make_async_copy(src, dst, load.at[i])
        for i, (src, dst) in enumerate(
            (
                (f2_in, fbuf.at[0, own_chunk]), (p2_in, p2), (go_in, go), (p1_in, p1),
                (xin_in, xin), (f1_in, fbuf.at[1, own_chunk]),
            )
        )
    ]
    for copy in loads:
        copy.start()

    for f in range(2):
        for x in range(xs + 2):
            for y in (0, ys + 1):
                gext[f, x, y] = jnp.zeros((zs, ch), jnp.bfloat16)
                gcat[f, x, y] = jnp.zeros((zs, 3 * ch), jnp.bfloat16)

    def gather_spread(f, got, which):
        for k in range(hi - 1, 0, -1):
            push(
                got, got, agz_s.at[f, which, k], agz_r.at[f, which, top],
                owner(near(k), mid, core),
            )

    def gather_own(f):
        mine = fbuf.at[f, own_chunk]
        push(mine, mine, agx_s.at[f], agx_r.at[f], across)

        @pl.when(lead)
        def _():
            gather_spread(f, mine, 0)

        push(mine, mine, agc_s.at[f, 0], agc_r.at[f, mid * hi + top], partner)

    def hand_on(f, got, t, m, k, cross=True):
        if cross:
            push(got, got, agy_s.at[f, k], agy_r.at[f, m * hi + t], me, 1 - group)
        push(got, got, agc_s.at[f, k], agc_r.at[f, m * hi + t], partner)

    def gather_side(f):
        got = fbuf.at[f, chunk(top, 1 - mid, core)]
        arrive(got, agx_r.at[f])

        @pl.when(lead)
        def _():
            gather_spread(f, got, 1)

        hand_on(f, got, top, 1 - mid, hi, False)

    def gather_line(f, side):
        @pl.when(lead)
        def _():
            for k in range(1, hi):
                t = near(k)
                which = 1 - mid if side else mid
                got = fbuf.at[f, chunk(t, which, core)]
                arrive(got, agz_r.at[f, side, t])
                hand_on(f, got, t, which, side * hi + k)

    def gather_follow(f):
        @pl.when(follower)
        def _():
            for half in range(2):
                which = mid + half * (1 - 2 * mid)
                for k in range(1, hi):
                    t = near(k)
                    got = fbuf.at[f, chunk(t, which, core)]
                    arrive(got, agy_r.at[f, which * hi + t])
                    hand_on(f, got, t, which, half * hi + k, False)

    def gather_core(f):
        for m in range(2):
            for t in range(hi):
                arrive(fbuf.at[f, chunk(t, m, 1 - core)], agc_r.at[f, m * hi + t])
        taps = 3 * ch // sub
        for ab in range(9):
            rows = fbuf[f, ab * taps : (ab + 1) * taps].astype(jnp.float32)
            wbuf[f, :, ab * ch : (ab + 1) * ch] = rows.reshape(3 * ch, ch).astype(jnp.bfloat16)

    def halo_copy(h, first, last, low, high):
        to_left = remote(
            first, high, halo_s.at[h, 0], halo_r.at[h, 1], lax.rem(me + n - 1, n), group
        )
        to_right = remote(
            last, low, halo_s.at[h, 1], halo_r.at[h, 0], lax.rem(me + 1, n), group
        )

        @pl.when(me > 0)
        def _():
            to_left.start()

        @pl.when(me < n - 1)
        def _():
            to_right.start()

        return to_left, to_right, low, high, h

    def halo_wait(halo):
        _, _, low, high, h = halo

        @pl.when(me > 0)
        def _():
            arrive(low, halo_r.at[h, 0])

        @pl.when(me == 0)
        def _():
            low[...] = jnp.zeros(low.shape, low.dtype)

        @pl.when(me < n - 1)
        def _():
            arrive(high, halo_r.at[h, 1])

        @pl.when(me == n - 1)
        def _():
            high[...] = jnp.zeros(high.shape, high.dtype)

    def grad_halo(f):
        inner = pl.ds(1, ys)
        return halo_copy(
            f, gext.at[f, 1, inner], gext.at[f, xs, inner],
            gext.at[f, 0, inner], gext.at[f, xs + 1, inner],
        )

    def keep_shifts(f, x, y, value):
        for c in (-1, 0, 1):
            gcat[f, x + 1, y + 1, :, (c + 1) * ch : (c + 2) * ch] = shift_z(value, c).astype(
                jnp.bfloat16
            )

    def keep_grad(f, x, y, value):
        gext[f, x + 1, y + 1] = value.astype(jnp.bfloat16)
        keep_shifts(f, x, y, value)

    def halo_shifts(f):
        for x in (-1, xs):
            for y in range(ys):
                keep_shifts(f, x, y, gext[f, x + 1, y + 1].astype(jnp.float32))

    def turn(s, layer, block):
        for y in range(ys):
            sat[s, layer, :, y * zs : (y + 1) * zs] = block[y].T

    per = ch // sub

    def filter_terms(s, a):
        lhs = jnp.concatenate([sat[s, x] for x in range(xs)], axis=1)
        for b in (-1, 0, 1):
            rhs = gcat[s, pl.ds(2 - a, xs), 1 - b : 1 - b + ys].reshape(xs * ys * zs, 3 * ch)
            out = jnp.dot(lhs, rhs, preferred_element_type=jnp.float32)
            for c in range(3):
                part[s, pl.ds((9 * a + 3 * (b + 1) + c) * per, per)] = out[
                    :, c * ch : (c + 1) * ch
                ].reshape(per, sub, ch)

    def scatter_core(s, i):
        t = from_far(i)
        for m in range(2):
            which = 1 - mid if m == 0 else mid
            s1[s, m, t] = part[s, chunk(t, which, 1 - core)].astype(jnp.bfloat16)
            push(s1.at[s, m, t], r1.at[s, m, t], rs1_s.at[s, m, i], rs1_r.at[s, m, t], partner)

    def terms_out(s):
        for j in range(3):
            filter_terms(s, (1 - upper) * (2 - j) + upper * j)
            for i in range(j * hi // 3, (j + 1) * hi // 3):
                scatter_core(s, i)

    def scatter_mid(s, steps):
        for i in steps:
            t = far_peer(i) if i < hi - 1 else top
            arrive(r1.at[s, 0, t], rs1_r.at[s, 0, t])
            s2[s, t] = (
                part[s, chunk(t, 1 - mid, core)] + r1[s, 0, t].astype(jnp.float32)
            ).astype(jnp.bfloat16)
            push(s2.at[s, t], r2.at[s, t], rs2_s.at[s, i], rs2_r.at[s, t], across)

    def total(s, t):
        arrive(r1.at[s, 1, t], rs1_r.at[s, 1, t])
        arrive(r2.at[s, t], rs2_r.at[s, t])
        return (
            part[s, chunk(t, mid, core)]
            + r1[s, 1, t].astype(jnp.float32)
            + r2[s, t].astype(jnp.float32)
        )

    def scatter_top(s):
        for i in range(hi - 1):
            t = far_peer(i)
            s3[s, t] = total(s, t).astype(jnp.bfloat16)
            push(
                s3.at[s, t], r3.at[s, top], rs3_s.at[s, i], rs3_r.at[s, top],
                owner(t, mid, core),
            )

    def scatter_end(s, out):
        value = total(s, top)
        for i in range(hi - 1, 0, -1):
            t = near(i)
            arrive(r3.at[s, t], rs3_r.at[s, t])
            value = value + r3[s, t].astype(jnp.float32)
        out[...] = value * grad_scale

    def layer_back(f, x):
        lhs = jnp.concatenate(
            [
                gext[f, x + 1 - a, 1 - b : 1 - b + ys].reshape(ys * zs, ch)
                for a in (-1, 0, 1)
                for b in (-1, 0, 1)
            ],
            axis=1,
        )
        wide = lax.dot_general(
            lhs, wbuf[f], (((1,), (1,)), ((), ())), preferred_element_type=jnp.float32
        )
        rows = []
        for y in range(ys):
            block = wide[y * zs : (y + 1) * zs]
            rows.append(
                shift_z(block[:, :ch], -1) + block[:, ch : 2 * ch] + shift_z(block[:, 2 * ch :], 1)
            )
        return rows

    pl.semaphore_wait(barrier, len(peers) + 1)
    loads[0].wait()
    gather_own(0)
    loads[1].wait()
    loads[2].wait()

    @pl.loop(0, xs * ys)
    def _(i):
        x, y = i // ys, i % ys
        _, slope_two = gelu_parts(p2[x, y].astype(jnp.float32))
        keep_grad(0, x, y, go[x, y].astype(jnp.float32) * slope_two)

    halo_two = grad_halo(0)
    loads[3].wait()

    @pl.loop(0, xs * ys)
    def _(i):
        x, y = i // ys, i % ys
        act, slope_one = gelu_parts(p1[x, y].astype(jnp.float32))
        abuf[x, y] = act.astype(jnp.bfloat16)
        slope[x, y] = slope_one

    loads[4].wait()
    for x in range(xs):
        turn(0, x, abuf[x])
        turn(1, x, xin[x])
    loads[5].wait()
    gather_side(0)
    gather_line(0, 0)
    gather_line(0, 1)
    gather_own(1)
    halo_wait(halo_two)
    halo_shifts(0)
    terms_out(0)
    gather_side(1)
    gather_follow(0)
    scatter_mid(0, range(hi // 2))
    gather_core(0)
    for x in range(xs):
        for y, value in enumerate(layer_back(0, x)):
            keep_grad(1, x, y, value * slope[x, y])
    halo_one = grad_halo(1)
    scatter_mid(0, range(hi // 2, hi))
    gather_line(1, 0)
    gather_line(1, 1)
    scatter_top(0)
    halo_wait(halo_one)
    halo_shifts(1)
    terms_out(1)
    scatter_mid(1, range(hi))
    gather_follow(1)
    gather_core(1)
    for x in range(xs):
        for y, value in enumerate(layer_back(1, x)):
            gin[x, y] = value.astype(jnp.bfloat16)
    scatter_top(1)
    scatter_end(0, own2)
    scatter_end(1, own1)

    def left(send):
        remote(
            fbuf.at[0, own_chunk], fbuf.at[0, own_chunk], send, agc_r.at[0, 0], partner, group
        ).wait_send()

    for f in range(2):
        left(agx_s.at[f])
        left(agc_s.at[f, 0])
        for k in range(1, 2 * hi):
            left(agc_s.at[f, k])

        @pl.when(lead)
        def _():
            for k in range(1, hi):
                left(agz_s.at[f, 0, k])
                left(agz_s.at[f, 1, k])
                left(agy_s.at[f, k])
                left(agy_s.at[f, hi + k])

        for i in range(hi):
            for m in range(2):
                left(rs1_s.at[f, m, i])
            left(rs2_s.at[f, i])
        for i in range(hi - 1):
            left(rs3_s.at[f, i])

    for halo in (halo_two, halo_one):

        @pl.when(me > 0)
        def _():
            halo[0].wait_send()

        @pl.when(me < n - 1)
        def _():
            halo[1].wait_send()


def store_kernel(*refs):
    count = (len(refs) - 1) // 2
    copies = [
        pltpu.make_async_copy(refs[i], refs[count + i], refs[-1].at[i]) for i in range(count)
    ]
    for copy in copies:
        copy.start()
    for copy in copies:
        copy.wait()


def store_out(*results):
    return pl.pallas_call(
        store_kernel,
        out_shape=tuple(jax.ShapeDtypeStruct(r.shape, r.dtype) for r in results),
        in_specs=[pl.BlockSpec(memory_space=pltpu.VMEM)] * len(results),
        out_specs=[pl.BlockSpec(memory_space=pl.ANY)] * len(results),
        scratch_shapes=[pltpu.SemaphoreType.DMA((len(results),))],
    )(*(pltpu.with_memory_space_constraint(r, pltpu.VMEM) for r in results))


def fused(grad_out, inputs, pre_first, pre_second, filter_first, filter_second):
    n = lax.axis_size("gx")
    xs, ys, zs, ch = grad_out.shape
    rows = filter_first.shape[0]
    if rows % sub or n % 4 or n < 8 or lax.axis_size("groups") != 2:
        return on_device(grad_out, inputs, pre_first, pre_second, filter_first, filter_second)
    units, hi, bf = rows // sub, n // 4, jnp.bfloat16
    dma = pltpu.SemaphoreType.DMA
    piece = (units, sub, ch)
    block = pltpu.VMEM((xs, ys, zs, ch), bf)
    gin, own1, own2 = pl.pallas_call(
        functools.partial(kernel, n),
        out_shape=(
            pltpu.VMEM(grad_out.shape, bf),
            pltpu.VMEM(piece, jnp.float32),
            pltpu.VMEM(piece, jnp.float32),
        ),
        in_specs=[pl.BlockSpec(memory_space=pl.ANY)] * 6,
        out_specs=[pl.BlockSpec(memory_space=pltpu.VMEM)] * 3,
        scratch_shapes=[
            block, block, block, block,
            pltpu.VMEM((2, n * units, sub, ch), bf),
            pltpu.VMEM((2, 3 * ch, 9 * ch), bf),
            pltpu.VMEM((2, xs + 2, ys + 2, zs, ch), bf),
            block,
            pltpu.VMEM((2, xs, ch, ys * zs), bf),
            pltpu.VMEM((2, xs + 2, ys + 2, zs, 3 * ch), bf),
            pltpu.VMEM((xs, ys, zs, ch), jnp.float32),
            pltpu.VMEM((2, n * units, sub, ch), jnp.float32),
            pltpu.VMEM((2, 2, hi) + piece, bf),
            pltpu.VMEM((2, 2, hi) + piece, bf),
            pltpu.VMEM((2, hi) + piece, bf),
            pltpu.VMEM((2, hi) + piece, bf),
            pltpu.VMEM((2, hi) + piece, bf),
            pltpu.VMEM((2, hi) + piece, bf),
            dma((6,)),
            dma((2, 2)), dma((2, 2)),
            dma((2, 2, hi)), dma((2, 2, hi)),
            dma((2,)), dma((2,)),
            dma((2, 2 * hi)), dma((2, 2 * hi)),
            dma((2, 2 * hi)), dma((2, 2 * hi)),
            dma((2, 2, hi)), dma((2, 2, hi)),
            dma((2, hi)), dma((2, hi)),
            dma((2, hi)), dma((2, hi)),
        ],
        compiler_params=pltpu.CompilerParams(collective_id=0, has_side_effects=True),
    )(
        grad_out, inputs, pre_first, pre_second,
        filter_first.reshape(piece), filter_second.reshape(piece),
    )
    gin, own1, own2 = store_out(gin, own1, own2)
    return gin, own1.reshape(rows, ch), own2.reshape(rows, ch)


def solution(mesh):
    return jax.shard_map(
        fused,
        mesh=mesh,
        in_specs=(
            P(("groups", "gx"), None, None, None),
            P(("groups", "gx"), None, None, None),
            P(("groups", "gx"), None, None, None),
            P(("groups", "gx"), None, None, None),
            P("gx", None),
            P("gx", None),
        ),
        out_specs=(P(("groups", "gx"), None, None, None), P("gx", "groups"), P("gx", "groups")),
        check_vma=False,
    )
```

time: 43.9 us -> 40.5 us (0.923)
  other arithmetic: 2.53 us -> 0 us
  Pallas kernels: 40.5 us -> 39.7 us
    convert_element_type x1 -> x0, other arithmetic: 1.83 us -> none  [fused(): gin.astype(bf)]
    pallas_call x1 -> x2, Pallas kernels: 40.5 us -> 39.7 us  [the longest x1 38.9 us: fused(): pl.pallas_call(functools.partial(kernel, n), out_shape=(pltpu.VMEM(grad_o...]
    mul x1 -> x0, other arithmetic: 0.7 us -> none  [fused(): own2.reshape(rows, ch) * scale]
where the time goes in v1:
time: 40.5 us; the launch traced here: 40.4 us
  Pallas kernels  39.7 us (98%)
  between operations  0.64 us (2%)
    pallas_call x1, Pallas kernels, fused(): pl.pallas_call(functools.partial(kernel, n), out_shape=(pltpu.VMEM(grad_o...  38.9 us

profile of v1, /device:TPU:0, one launch (start us, length us, event | category | flops | bytes accessed | tf_op | source)
XLA Modules:
  0.0 40.4 jit_solution(15912199004203382875)
XLA Ops:
  0.6 38.9 %shard_map.85 = (bf16[2,4,128,128]{3,2,1,0:T(8,128)(2,1)S(1)}, f32[27,8,128]{2,1,0:T(8,128)S(1)}, f32[27,8,128]{2,1,0:T(8,128)S(1)}) custom-call(bf16[2,4,128,128]{3,2,1,0:T(8,128)(2,1)} %go_in.1, bf16[2,4,128,128]{3,2,1,0:T(8,128)(2,1)} %xin_in.1, bf16[2,4,128,128]{3,2,1,0:T(8,128)(2,1)} %p1_in.1, bf16[2,4,128,128]{3,2,1,0:T(8,128)(2,1)} %p2_in.1, ...), custom_call_target="tpu_custom_call" | custom-call | tf_op jit(solution)/shard_map/pallas_call | solution.py:534
  39.6 0.8 %shard_map.86 = (bf16[2,4,128,128]{3,2,1,0:T(8,128)(2,1)}, f32[27,8,128]{2,1,0:T(8,128)}, f32[27,8,128]{2,1,0:T(8,128)}) custom-call(bf16[2,4,128,128]{3,2,1,0:T(8,128)(2,1)S(1)} %get-tuple-element.9.refs_0_, f32[27,8,128]{2,1,0:T(8,128)S(1)} %get-tuple-element.10.refs_1_, f32[27,8,128]{2,1,0:T(8,128)S(1)} %get-tuple-element.11.refs_2_), custom_call_target="tpu_custom_call" | custom-call | tf_op jit(solution)/shard_map/pallas_call | solution.py:515

commit v2 on v1

--- a/solution.py
+++ b/solution.py
@@ -121,9 +121,9 @@
 def kernel(
     n, go_in, xin_in, p1_in, p2_in, f1_in, f2_in, gin, own1, own2,
     go, xin, p1, p2,
-    fbuf, wbuf, gext, abuf, sat, gcat, slope, part, s1, r1, s2, r2, s3, r3,
-    load, halo_s, halo_r, agz_s, agz_r, agx_s, agx_r, agy_s, agy_r, agc_s, agc_r,
-    rs1_s, rs1_r, rs2_s, rs2_r, rs3_s, rs3_r,
+    fbuf, wbuf, gext, abuf, ahalo, sat, turned, gcat, slope, part, s1, r1, s2, r2, s3, r3, rg, s4, r4, rh,
+    load, halo_s, halo_r, sent, line_r, relay_r, cross_r, core_r, late_r,
+    rs1_r, rs2_r, rs3_r, rsg_r,
 ):
     xs, ys, zs, ch = go.shape
     units = f1_in.shape[0]
@@ -140,6 +140,10 @@
     upper = top // ((hi + 1) // 2)
     room = top + upper * (hi - 1 - 2 * top)
     place = top + (1 - upper) * (hi - 1 - 2 * top)
+    near_side = far = hi // 2
+    gate = far - 1 + upper
+    outer = top != gate
+    gate_slot = (top - gate - 1) % near_side
 
     def owner(t, m, c):
         return (t * 2 + m) * 2 + c
@@ -158,6 +162,9 @@
     def from_far(i):
         return (1 - upper) * (hi - 1 - i) + upper * i
 
+    def same_side(k):
+        return upper * far + (top - upper * far + k) % near_side
+
     def far_peer(i):
         return from_far(i + at_least(i + 1, place + 1))
 
@@ -167,11 +174,14 @@
             device_id=(plane, target), device_id_type=MESH,
         )
 
-    def push(src, dst, send, recv, target, plane=group):
-        remote(src, dst, send, recv, target, plane).start()
+    def push(src, dst, count, recv, target, plane=group):
+        remote(src, dst, sent.at[count], recv, target, plane).start()
 
     def arrive(dst, recv):
-        remote(dst, dst, halo_s.at[0, 0], recv, partner, group).wait_recv()
+        remote(dst, dst, sent.at[0], recv, partner, group).wait_recv()
+
+    def pieces(f, count):
+        return fbuf.at[f, pl.ds(0, count * units)]
 
     barrier = pltpu.get_barrier_semaphore()
     peers = [partner, across, lax.rem(me + 1, n), lax.rem(me + n - 1, n)]
@@ -199,63 +209,107 @@
                 gext[f, x, y] = jnp.zeros((zs, ch), jnp.bfloat16)
                 gcat[f, x, y] = jnp.zeros((zs, 3 * ch), jnp.bfloat16)
 
-    def gather_spread(f, got, which):
-        for k in range(hi - 1, 0, -1):
-            push(
-                got, got, agz_s.at[f, which, k], agz_r.at[f, which, top],
-                owner(near(k), mid, core),
-            )
-
-    def gather_own(f):
-        mine = fbuf.at[f, own_chunk]
-        push(mine, mine, agx_s.at[f], agx_r.at[f], across)
+    for x in range(xs + 2):
+        for y in (0, ys + 1):
+            turned[x, :, y * zs : (y + 1) * zs] = jnp.zeros((ch, zs), jnp.bfloat16)
+
+    def mine(f):
+        return fbuf.at[f, own_chunk]
+
+    def to_partner(f, got):
+        push(got, got, 3 * f, core_r.at[f], partner)
+
+    def cross(f, got, recv):
+        push(got, got, 4 + f, recv, me, 1 - group)
+        to_partner(f, got)
+
+    def first_own():
+        push(mine(0), mine(0), 0, relay_r.at[top], across)
 
         @pl.when(lead)
         def _():
-            gather_spread(f, mine, 0)
-
-        push(mine, mine, agc_s.at[f, 0], agc_r.at[f, mid * hi + top], partner)
-
-    def hand_on(f, got, t, m, k, cross=True):
-        if cross:
-            push(got, got, agy_s.at[f, k], agy_r.at[f, m * hi + t], me, 1 - group)
-        push(got, got, agc_s.at[f, k], agc_r.at[f, m * hi + t], partner)
-
-    def gather_side(f):
-        got = fbuf.at[f, chunk(top, 1 - mid, core)]
-        arrive(got, agx_r.at[f])
-
-        @pl.when(lead)
-        def _():
-            gather_spread(f, got, 1)
-
-        hand_on(f, got, top, 1 - mid, hi, False)
-
-    def gather_line(f, side):
+            for k in range(hi - 1, 0, -1):
+                push(mine(0), mine(0), 4, line_r.at[top], owner(near(k), mid, core))
+
+        to_partner(0, mine(0))
+
+    def first_side():
+        got = fbuf.at[0, chunk(top, 1 - mid, core)]
+        arrive(got, relay_r.at[top])
+        to_partner(0, got)
+
+    def first_line():
         @pl.when(lead)
         def _():
             for k in range(1, hi):
                 t = near(k)
+                got = fbuf.at[0, chunk(t, mid, core)]
+                arrive(got, line_r.at[t])
+                push(got, got, 4, relay_r.at[t], across)
+                cross(0, got, cross_r.at[mid * hi + t])
+
+    def first_relay():
+        @pl.when(lead)
+        def _():
+            for k in range(1, hi):
+                t = near(k)
+                got = fbuf.at[0, chunk(t, 1 - mid, core)]
+                arrive(got, relay_r.at[t])
+                cross(0, got, cross_r.at[(1 - mid) * hi + t])
+
+    def first_follow():
+        @pl.when(follower)
+        def _():
+            for side in range(2):
                 which = 1 - mid if side else mid
-                got = fbuf.at[f, chunk(t, which, core)]
-                arrive(got, agz_r.at[f, side, t])
-                hand_on(f, got, t, which, side * hi + k)
-
-    def gather_follow(f):
-        @pl.when(follower)
-        def _():
-            for half in range(2):
-                which = mid + half * (1 - 2 * mid)
                 for k in range(1, hi):
                     t = near(k)
-                    got = fbuf.at[f, chunk(t, which, core)]
-                    arrive(got, agy_r.at[f, which * hi + t])
-                    hand_on(f, got, t, which, half * hi + k, False)
+                    got = fbuf.at[0, chunk(t, which, core)]
+                    arrive(got, cross_r.at[which * hi + t])
+                    to_partner(0, got)
+
+    def late_own():
+        to_partner(1, mine(1))
+
+        @pl.when(lead)
+        def _():
+            push(mine(1), mine(1), 5, late_r.at[0], across)
+
+    def late_spread():
+        @pl.when(lead)
+        def _():
+            for k in range(hi - 1, 0, -1):
+                push(mine(1), mine(1), 5, late_r.at[1], owner(near(k), mid, core))
+
+    def late_line():
+        @pl.when(lead)
+        def _():
+            arrive(pieces(1, hi - 1), late_r.at[1])
+            for k in range(1, hi):
+                got = fbuf.at[1, chunk(near(k), mid, core)]
+                push(got, got, 5, late_r.at[2], across)
+                cross(1, got, late_r.at[3])
+
+    def late_relay():
+        @pl.when(lead)
+        def _():
+            arrive(mine(1), late_r.at[0])
+            arrive(pieces(1, hi - 1), late_r.at[2])
+            for k in range(hi):
+                t = near(k) if k else top
+                cross(1, fbuf.at[1, chunk(t, 1 - mid, core)], late_r.at[3])
+
+    def late_follow():
+        @pl.when(follower)
+        def _():
+            arrive(pieces(1, 2 * hi - 1), late_r.at[3])
+            to_partner(1, fbuf.at[1, chunk(top, 1 - mid, core)])
+            for k in range(1, hi):
+                for m in range(2):
+                    to_partner(1, fbuf.at[1, chunk(near(k), m, core)])
 
     def gather_core(f):
-        for m in range(2):
-            for t in range(hi):
-                arrive(fbuf.at[f, chunk(t, m, 1 - core)], agc_r.at[f, m * hi + t])
+        arrive(pieces(f, 2 * hi), core_r.at[f])
         taps = 3 * ch // sub
         for ab in range(9):
             rows = fbuf[f, ab * taps : (ab + 1) * taps].astype(jnp.float32)
@@ -263,10 +317,10 @@
 
     def halo_copy(h, first, last, low, high):
         to_left = remote(
-            first, high, halo_s.at[h, 0], halo_r.at[h, 1], lax.rem(me + n - 1, n), group
+            first, high, halo_s.at[0], halo_r.at[h, 1], lax.rem(me + n - 1, n), group
         )
         to_right = remote(
-            last, low, halo_s.at[h, 1], halo_r.at[h, 0], lax.rem(me + 1, n), group
+            last, low, halo_s.at[1], halo_r.at[h, 0], lax.rem(me + 1, n), group
         )
 
         @pl.when(me > 0)
@@ -277,10 +331,10 @@
         def _():
             to_right.start()
 
-        return to_left, to_right, low, high, h
+        return low, high, h
 
     def halo_wait(halo):
-        _, _, low, high, h = halo
+        low, high, h = halo
 
         @pl.when(me > 0)
         def _():
@@ -305,6 +359,9 @@
             gext.at[f, 0, inner], gext.at[f, xs + 1, inner],
         )
 
+    def saved_halo(h, block):
+        return halo_copy(h, block.at[0], block.at[xs - 1], ahalo.at[0], ahalo.at[1])
+
     def keep_shifts(f, x, y, value):
         for c in (-1, 0, 1):
             gcat[f, x + 1, y + 1, :, (c + 1) * ch : (c + 2) * ch] = shift_z(value, c).astype(
@@ -320,9 +377,13 @@
             for y in range(ys):
                 keep_shifts(f, x, y, gext[f, x + 1, y + 1].astype(jnp.float32))
 
-    def turn(s, layer, block):
+    def turn(layer, block):
         for y in range(ys):
-            sat[s, layer, :, y * zs : (y + 1) * zs] = block[y].T
+            sat[0, layer, :, y * zs : (y + 1) * zs] = block[y].T
+
+    def turn_input(layer, block):
+        for y in range(ys):
+            turned[layer, :, (y + 1) * zs : (y + 2) * zs] = block[y].T
 
     per = ch // sub
 
@@ -336,53 +397,145 @@
                     :, c * ch : (c + 1) * ch
                 ].reshape(per, sub, ch)
 
+    def filter_terms_dense(s, a):
+        lhs = jnp.concatenate(
+            [
+                jnp.concatenate(
+                    [turned[x + a, :, b * zs : (b + ys) * zs] for x in range(xs)], axis=1
+                )
+                for b in range(3)
+            ],
+            axis=0,
+        )
+        rhs = gcat[s, 1 : xs + 1, 1 : ys + 1].reshape(xs * ys * zs, 3 * ch)
+        out = jnp.dot(lhs, rhs, preferred_element_type=jnp.float32)
+        for b in range(3):
+            for c in range(3):
+                part[s, pl.ds((9 * a + 3 * b + c) * per, per)] = out[
+                    b * ch : (b + 1) * ch, c * ch : (c + 1) * ch
+                ].reshape(per, sub, ch)
+
+    def side_of(j):
+        return mid if j else 1 - mid
+
     def scatter_core(s, i):
         t = from_far(i)
-        for m in range(2):
-            which = 1 - mid if m == 0 else mid
-            s1[s, m, t] = part[s, chunk(t, which, 1 - core)].astype(jnp.bfloat16)
-            push(s1.at[s, m, t], r1.at[s, m, t], rs1_s.at[s, m, i], rs1_r.at[s, m, t], partner)
-
-    def terms_out(s):
-        for j in range(3):
-            filter_terms(s, (1 - upper) * (2 - j) + upper * j)
+        for j in range(2):
+            s1[s, t, j] = part[s, chunk(t, side_of(j), 1 - core)].astype(jnp.bfloat16)
+            if s:
+                push(s1.at[s, t, j], r1.at[s, t, j], 1 + s, rs1_r.at[s, hi if j else t], partner)
+        if not s:
+            push(s1.at[s, t], r1.at[s, t], 1 + s, rs1_r.at[s, t], partner)
+
+    def terms_out(s, steps=range(3)):
+        for j in steps:
+            (filter_terms_dense if s else filter_terms)(s, (1 - upper) * (2 - j) + upper * j)
             for i in range(j * hi // 3, (j + 1) * hi // 3):
                 scatter_core(s, i)
 
-    def scatter_mid(s, steps):
-        for i in steps:
+    def cell(t, j):
+        return chunk(t, side_of(j), core)
+
+    def pair_sum(t):
+        arrive(r1.at[0, t], rs1_r.at[0, t])
+        return [part[0, cell(t, j)] + r1[0, t, j].astype(jnp.float32) for j in range(2)]
+
+    def line_send(t, values, dst, recv, target):
+        for j in range(2):
+            s3[t, j] = values[j].astype(jnp.bfloat16)
+        push(s3.at[t], dst, 1, recv, owner(target, mid, core))
+
+    def line_out():
+        for i in range(far):
+            t = from_far(i)
+            values = pair_sum(t)
+
+            @pl.when(outer)
+            def _():
+                line_send(t, values, rg.at[i, gate_slot], rsg_r.at[0, i], gate)
+
+            @pl.when(jnp.logical_not(outer))
+            def _():
+                for j in range(2):
+                    part[0, cell(t, j)] = values[j]
+
+        for k in range(1, near_side):
+            t = same_side(k)
+            line_send(t, pair_sum(t), r3.at[k - 1], rs3_r.at[0], t)
+
+    def line_gate():
+        @pl.when(jnp.logical_not(outer))
+        def _():
+            for i in range(far):
+                t = from_far(i)
+                arrive(rg.at[i, pl.ds(0, near_side - 1)], rsg_r.at[0, i])
+                values = [part[0, cell(t, j)] for j in range(2)]
+                for k in range(near_side - 1):
+                    values = [values[j] + rg[i, k, j].astype(jnp.float32) for j in range(2)]
+                line_send(t, values, r3.at[near_side - 1], rs3_r.at[0], t)
+
+    def line_end():
+        values = pair_sum(top)
+        arrive(r3, rs3_r.at[0])
+        for k in range(near_side):
+            values = [values[j] + r3[k, j].astype(jnp.float32) for j in range(2)]
+        part[0, own_chunk] = values[1]
+        s2[0, 0] = values[0].astype(jnp.bfloat16)
+        push(s2.at[0, 0], r2.at[0, 0], 1, rs2_r.at[0, 0], across)
+
+    def line_store():
+        arrive(r2.at[0, 0], rs2_r.at[0, 0])
+        own2[...] = (part[0, own_chunk] + r2[0, 0].astype(jnp.float32)) * grad_scale
+
+    def side_out():
+        for i in range(hi):
             t = far_peer(i) if i < hi - 1 else top
-            arrive(r1.at[s, 0, t], rs1_r.at[s, 0, t])
-            s2[s, t] = (
-                part[s, chunk(t, 1 - mid, core)] + r1[s, 0, t].astype(jnp.float32)
-            ).astype(jnp.bfloat16)
-            push(s2.at[s, t], r2.at[s, t], rs2_s.at[s, i], rs2_r.at[s, t], across)
-
-    def total(s, t):
-        arrive(r1.at[s, 1, t], rs1_r.at[s, 1, t])
-        arrive(r2.at[s, t], rs2_r.at[s, t])
+            arrive(r1.at[1, t, 0], rs1_r.at[1, t])
+            s2[1, t] = (part[1, cell(t, 0)] + r1[1, t, 0].astype(jnp.float32)).astype(
+                jnp.bfloat16
+            )
+            push(s2.at[1, t], r2.at[1, t], 2, rs2_r.at[1, t], across)
+
+    def total(t):
+        arrive(r2.at[1, t], rs2_r.at[1, t])
         return (
-            part[s, chunk(t, mid, core)]
-            + r1[s, 1, t].astype(jnp.float32)
-            + r2[s, t].astype(jnp.float32)
-        )
-
-    def scatter_top(s):
-        for i in range(hi - 1):
-            t = far_peer(i)
-            s3[s, t] = total(s, t).astype(jnp.bfloat16)
-            push(
-                s3.at[s, t], r3.at[s, top], rs3_s.at[s, i], rs3_r.at[s, top],
-                owner(t, mid, core),
-            )
-
-    def scatter_end(s, out):
-        value = total(s, top)
-        for i in range(hi - 1, 0, -1):
-            t = near(i)
-            arrive(r3.at[s, t], rs3_r.at[s, t])
-            value = value + r3[s, t].astype(jnp.float32)
-        out[...] = value * grad_scale
+            part[1, cell(t, 1)]
+            + r1[1, t, 1].astype(jnp.float32)
+            + r2[1, t].astype(jnp.float32)
+        )
+
+    def send_last(t, value, dst, recv, target):
+        s4[t] = value.astype(jnp.bfloat16)
+        push(s4.at[t], dst, 2, recv, owner(target, mid, core))
+
+    def side_line():
+        arrive(fbuf.at[0, pl.ds(0, hi * units)], rs1_r.at[1, hi])
+        for i in range(far):
+            t = from_far(i)
+            value = total(t)
+
+            @pl.when(outer)
+            def _():
+                send_last(t, value, rh.at[i, gate_slot], rsg_r.at[1, i], gate)
+
+            @pl.when(jnp.logical_not(outer))
+            def _():
+                arrive(rh.at[i, pl.ds(0, near_side - 1)], rsg_r.at[1, i])
+                merged = value
+                for k in range(near_side - 1):
+                    merged = merged + rh[i, k].astype(jnp.float32)
+                send_last(t, merged, r4.at[near_side - 1], rs3_r.at[1], t)
+
+        for k in range(1, near_side):
+            t = same_side(k)
+            send_last(t, total(t), r4.at[k - 1], rs3_r.at[1], t)
+
+    def side_store():
+        value = total(top)
+        arrive(r4, rs3_r.at[1])
+        for k in range(near_side):
+            value = value + r4[k].astype(jnp.float32)
+        own1[...] = value * grad_scale
 
     def layer_back(f, x):
         lhs = jnp.concatenate(
@@ -406,7 +559,7 @@
 
     pl.semaphore_wait(barrier, len(peers) + 1)
     loads[0].wait()
-    gather_own(0)
+    first_own()
     loads[1].wait()
     loads[2].wait()
 
@@ -428,76 +581,64 @@
 
     loads[4].wait()
     for x in range(xs):
-        turn(0, x, abuf[x])
-        turn(1, x, xin[x])
+        turn(x, abuf[x])
+        turn_input(x + 1, xin[x])
     loads[5].wait()
-    gather_side(0)
-    gather_line(0, 0)
-    gather_line(0, 1)
-    gather_own(1)
+    first_line()
+    late_own()
+    late_spread()
+    halo_in = saved_halo(2, xin)
+    first_side()
     halo_wait(halo_two)
     halo_shifts(0)
     terms_out(0)
-    gather_side(1)
-    gather_follow(0)
-    scatter_mid(0, range(hi // 2))
+    first_relay()
+    line_out()
+    late_line()
+    first_follow()
     gather_core(0)
     for x in range(xs):
         for y, value in enumerate(layer_back(0, x)):
             keep_grad(1, x, y, value * slope[x, y])
     halo_one = grad_halo(1)
-    scatter_mid(0, range(hi // 2, hi))
-    gather_line(1, 0)
-    gather_line(1, 1)
-    scatter_top(0)
+    line_gate()
+    late_relay()
+    halo_wait(halo_in)
+    turn_input(0, ahalo[0])
+    turn_input(xs + 1, ahalo[1])
+    terms_out(1)
+    side_out()
+    late_follow()
     halo_wait(halo_one)
-    halo_shifts(1)
-    terms_out(1)
-    scatter_mid(1, range(hi))
-    gather_follow(1)
     gather_core(1)
     for x in range(xs):
         for y, value in enumerate(layer_back(1, x)):
             gin[x, y] = value.astype(jnp.bfloat16)
-    scatter_top(1)
-    scatter_end(0, own2)
-    scatter_end(1, own1)
-
-    def left(send):
-        remote(
-            fbuf.at[0, own_chunk], fbuf.at[0, own_chunk], send, agc_r.at[0, 0], partner, group
-        ).wait_send()
-
-    for f in range(2):
-        left(agx_s.at[f])
-        left(agc_s.at[f, 0])
-        for k in range(1, 2 * hi):
-            left(agc_s.at[f, k])
-
-        @pl.when(lead)
-        def _():
-            for k in range(1, hi):
-                left(agz_s.at[f, 0, k])
-                left(agz_s.at[f, 1, k])
-                left(agy_s.at[f, k])
-                left(agy_s.at[f, hi + k])
-
-        for i in range(hi):
-            for m in range(2):
-                left(rs1_s.at[f, m, i])
-            left(rs2_s.at[f, i])
-        for i in range(hi - 1):
-            left(rs3_s.at[f, i])
-
-    for halo in (halo_two, halo_one):
-
-        @pl.when(me > 0)
-        def _():
-            halo[0].wait_send()
-
-        @pl.when(me < n - 1)
-        def _():
-            halo[1].wait_send()
+    line_end()
+    side_line()
+    line_store()
+    side_store()
+
+    def left(count, send):
+        remote(pieces(0, count), pieces(0, count), send, core_r.at[0], partner, group).wait_send()
+
+    for i, count in enumerate((2 * hi + 1, 4 * hi - 1, 4 * hi - 1, 2 * hi)):
+        left(count, sent.at[i])
+
+    @pl.when(lead)
+    def _():
+        left(4 * hi - 4, sent.at[4])
+        left(4 * hi - 2, sent.at[5])
+
+    layers = gext.at[0, pl.ds(0, 3), pl.ds(1, ys)]
+
+    @pl.when(me > 0)
+    def _():
+        remote(layers, layers, halo_s.at[0], core_r.at[0], partner, group).wait_send()
+
+    @pl.when(me < n - 1)
+    def _():
+        remote(layers, layers, halo_s.at[1], core_r.at[0], partner, group).wait_send()
 
 
 def store_kernel(*refs):
@@ -525,7 +666,7 @@
     n = lax.axis_size("gx")
     xs, ys, zs, ch = grad_out.shape
     rows = filter_first.shape[0]
-    if rows % sub or n % 4 or n < 8 or lax.axis_size("groups") != 2:
+    if rows % sub or n % 8 or n < 16 or lax.axis_size("groups") != 2:
         return on_device(grad_out, inputs, pre_first, pre_second, filter_first, filter_second)
     units, hi, bf = rows // sub, n // 4, jnp.bfloat16
     dma = pltpu.SemaphoreType.DMA
@@ -546,25 +687,25 @@
             pltpu.VMEM((2, 3 * ch, 9 * ch), bf),
             pltpu.VMEM((2, xs + 2, ys + 2, zs, ch), bf),
             block,
-            pltpu.VMEM((2, xs, ch, ys * zs), bf),
+            pltpu.VMEM((2, ys, zs, ch), bf),
+            pltpu.VMEM((1, xs, ch, ys * zs), bf),
+            pltpu.VMEM((xs + 2, ch, (ys + 2) * zs), bf),
             pltpu.VMEM((2, xs + 2, ys + 2, zs, 3 * ch), bf),
             pltpu.VMEM((xs, ys, zs, ch), jnp.float32),
             pltpu.VMEM((2, n * units, sub, ch), jnp.float32),
-            pltpu.VMEM((2, 2, hi) + piece, bf),
-            pltpu.VMEM((2, 2, hi) + piece, bf),
+            pltpu.VMEM((2, hi, 2) + piece, bf),
+            pltpu.VMEM((2, hi, 2) + piece, bf),
             pltpu.VMEM((2, hi) + piece, bf),
             pltpu.VMEM((2, hi) + piece, bf),
-            pltpu.VMEM((2, hi) + piece, bf),
-            pltpu.VMEM((2, hi) + piece, bf),
-            dma((6,)),
-            dma((2, 2)), dma((2, 2)),
-            dma((2, 2, hi)), dma((2, 2, hi)),
-            dma((2,)), dma((2,)),
-            dma((2, 2 * hi)), dma((2, 2 * hi)),
-            dma((2, 2 * hi)), dma((2, 2 * hi)),
-            dma((2, 2, hi)), dma((2, 2, hi)),
-            dma((2, hi)), dma((2, hi)),
-            dma((2, hi)), dma((2, hi)),
+            pltpu.VMEM((hi, 2) + piece, bf),
+            pltpu.VMEM((hi // 2, 2) + piece, bf),
+            pltpu.VMEM((hi // 2, hi // 2, 2) + piece, bf),
+            pltpu.VMEM((hi,) + piece, bf),
+            pltpu.VMEM((hi // 2,) + piece, bf),
+            pltpu.VMEM((hi // 2, hi // 2) + piece, bf),
+            dma((6,)), dma((2,)), dma((3, 2)), dma((6,)),
+            dma((hi,)), dma((hi,)), dma((2 * hi,)), dma((2,)), dma((4,)),
+            dma((2, hi + 1)), dma((2, hi)), dma((2,)), dma((2, hi // 2)),
         ],
         compiler_params=pltpu.CompilerParams(collective_id=0, has_side_effects=True),
     )(

time: 40.5 us -> 37 us (0.914)
  Pallas kernels: 39.7 us -> 36.2 us
    pallas_call x1, Pallas kernels: 38.9 us -> 35.5 us  [fused(): pl.pallas_call(functools.partial(kernel, n), out_shape=(pltpu.VMEM(grad_o...]
where the time goes in v2:
time: 37 us; the launch traced here: 36.9 us
  Pallas kernels  36.2 us (98%)
  between operations  0.64 us (2%)
    pallas_call x1, Pallas kernels, fused(): pl.pallas_call(functools.partial(kernel, n), out_shape=(pltpu.VMEM(grad_o...  35.5 us
    pallas_call x1, Pallas kernels, store_out(): pl.pallas_call(store_kernel, out_shape=tuple((jax.ShapeDtypeStruct(r.shap...  0.8 us

profile of v2, /device:TPU:0, one launch (start us, length us, event | category | flops | bytes accessed | tf_op | source)
XLA Modules:
  0.0 36.9 jit_solution(12963147433685916973)
XLA Ops:
  0.6 35.5 %shard_map.85 = (bf16[2,4,128,128]{3,2,1,0:T(8,128)(2,1)S(1)}, f32[27,8,128]{2,1,0:T(8,128)S(1)}, f32[27,8,128]{2,1,0:T(8,128)S(1)}) custom-call(bf16[2,4,128,128]{3,2,1,0:T(8,128)(2,1)} %go_in.1, bf16[2,4,128,128]{3,2,1,0:T(8,128)(2,1)} %xin_in.1, bf16[2,4,128,128]{3,2,1,0:T(8,128)(2,1)} %p1_in.1, bf16[2,4,128,128]{3,2,1,0:T(8,128)(2,1)} %p2_in.1, ...), custom_call_target="tpu_custom_call" | custom-call | tf_op jit(solution)/shard_map/pallas_call | solution.py:675
  36.1 0.8 %shard_map.86 = (bf16[2,4,128,128]{3,2,1,0:T(8,128)(2,1)}, f32[27,8,128]{2,1,0:T(8,128)}, f32[27,8,128]{2,1,0:T(8,128)}) custom-call(bf16[2,4,128,128]{3,2,1,0:T(8,128)(2,1)S(1)} %get-tuple-element.9.refs_0_, f32[27,8,128]{2,1,0:T(8,128)S(1)} %get-tuple-element.10.refs_1_, f32[27,8,128]{2,1,0:T(8,128)S(1)} %get-tuple-element.11.refs_2_), custom_call_target="tpu_custom_call" | custom-call | tf_op jit(solution)/shard_map/pallas_call | solution.py:656

commit v3 on v2

--- a/solution.py
+++ b/solution.py
@@ -487,8 +487,8 @@
         arrive(r2.at[0, 0], rs2_r.at[0, 0])
         own2[...] = (part[0, own_chunk] + r2[0, 0].astype(jnp.float32)) * grad_scale
 
-    def side_out():
-        for i in range(hi):
+    def side_out(steps):
+        for i in steps:
             t = far_peer(i) if i < hi - 1 else top
             arrive(r1.at[1, t, 0], rs1_r.at[1, t])
             s2[1, t] = (part[1, cell(t, 0)] + r1[1, t, 0].astype(jnp.float32)).astype(
@@ -587,12 +587,12 @@
     first_line()
     late_own()
     late_spread()
-    halo_in = saved_halo(2, xin)
     first_side()
     halo_wait(halo_two)
     halo_shifts(0)
     terms_out(0)
     first_relay()
+    halo_in = saved_halo(2, xin)
     line_out()
     late_line()
     first_follow()
@@ -600,22 +600,22 @@
     for x in range(xs):
         for y, value in enumerate(layer_back(0, x)):
             keep_grad(1, x, y, value * slope[x, y])
-    halo_one = grad_halo(1)
-    line_gate()
     late_relay()
     halo_wait(halo_in)
     turn_input(0, ahalo[0])
     turn_input(xs + 1, ahalo[1])
     terms_out(1)
-    side_out()
+    line_gate()
+    side_out(range(hi))
+    halo_one = grad_halo(1)
     late_follow()
+    side_line()
+    line_end()
     halo_wait(halo_one)
     gather_core(1)
     for x in range(xs):
         for y, value in enumerate(layer_back(1, x)):
             gin[x, y] = value.astype(jnp.bfloat16)
-    line_end()
-    side_line()
     line_store()
     side_store()
 

time: 37 us -> 35.7 us (0.965)
  Pallas kernels: 36.2 us -> 34.9 us
    pallas_call x1, Pallas kernels: 35.5 us -> 34.1 us  [fused(): pl.pallas_call(functools.partial(kernel, n), out_shape=(pltpu.VMEM(grad_o...]
where the time goes in v3:
time: 35.7 us; the launch traced here: 35.5 us
  Pallas kernels  34.9 us (98%)
  between operations  0.64 us (2%)
    pallas_call x1, Pallas kernels, fused(): pl.pallas_call(functools.partial(kernel, n), out_shape=(pltpu.VMEM(grad_o...  34.1 us
    pallas_call x1, Pallas kernels, store_out(): pl.pallas_call(store_kernel, out_shape=tuple((jax.ShapeDtypeStruct(r.shap...  0.8 us

profile of v3, /device:TPU:0, one launch (start us, length us, event | category | flops | bytes accessed | tf_op | source)
XLA Modules:
  0.0 35.5 jit_solution(16615435746415090908)
XLA Ops:
  0.6 34.1 %shard_map.85 = (bf16[2,4,128,128]{3,2,1,0:T(8,128)(2,1)S(1)}, f32[27,8,128]{2,1,0:T(8,128)S(1)}, f32[27,8,128]{2,1,0:T(8,128)S(1)}) custom-call(bf16[2,4,128,128]{3,2,1,0:T(8,128)(2,1)} %go_in.1, bf16[2,4,128,128]{3,2,1,0:T(8,128)(2,1)} %xin_in.1, bf16[2,4,128,128]{3,2,1,0:T(8,128)(2,1)} %p1_in.1, bf16[2,4,128,128]{3,2,1,0:T(8,128)(2,1)} %p2_in.1, ...), custom_call_target="tpu_custom_call" | custom-call | tf_op jit(solution)/shard_map/pallas_call | solution.py:675
  34.7 0.8 %shard_map.86 = (bf16[2,4,128,128]{3,2,1,0:T(8,128)(2,1)}, f32[27,8,128]{2,1,0:T(8,128)}, f32[27,8,128]{2,1,0:T(8,128)}) custom-call(bf16[2,4,128,128]{3,2,1,0:T(8,128)(2,1)S(1)} %get-tuple-element.9.refs_0_, f32[27,8,128]{2,1,0:T(8,128)S(1)} %get-tuple-element.10.refs_1_, f32[27,8,128]{2,1,0:T(8,128)S(1)} %get-tuple-element.11.refs_2_), custom_call_target="tpu_custom_call" | custom-call | tf_op jit(solution)/shard_map/pallas_call | solution.py:656

commit v4 on v3

--- a/solution.py
+++ b/solution.py
@@ -121,7 +121,7 @@
 def kernel(
     n, go_in, xin_in, p1_in, p2_in, f1_in, f2_in, gin, own1, own2,
     go, xin, p1, p2,
-    fbuf, wbuf, gext, abuf, ahalo, sat, turned, gcat, slope, part, s1, r1, s2, r2, s3, r3, rg, s4, r4, rh,
+    fbuf, wbuf, gext, abuf, ahalo, sat, turned, gcat, slope, part, s1, r1, s2, r2, s3, r3, rg, s4, r4,
     load, halo_s, halo_r, sent, line_r, relay_r, cross_r, core_r, late_r,
     rs1_r, rs2_r, rs3_r, rsg_r,
 ):
@@ -165,8 +165,8 @@
     def same_side(k):
         return upper * far + (top - upper * far + k) % near_side
 
-    def far_peer(i):
-        return from_far(i + at_least(i + 1, place + 1))
+    def low_peer(i):
+        return i + at_least(i + 1, top + 1)
 
     def remote(src, dst, send, recv, target, plane):
         return pltpu.make_async_remote_copy(
@@ -419,7 +419,7 @@
         return mid if j else 1 - mid
 
     def scatter_core(s, i):
-        t = from_far(i)
+        t = i if s else from_far(i)
         for j in range(2):
             s1[s, t, j] = part[s, chunk(t, side_of(j), 1 - core)].astype(jnp.bfloat16)
             if s:
@@ -429,7 +429,10 @@
 
     def terms_out(s, steps=range(3)):
         for j in steps:
-            (filter_terms_dense if s else filter_terms)(s, (1 - upper) * (2 - j) + upper * j)
+            if s:
+                filter_terms_dense(s, j)
+            else:
+                filter_terms(s, (1 - upper) * (2 - j) + upper * j)
             for i in range(j * hi // 3, (j + 1) * hi // 3):
                 scatter_core(s, i)
 
@@ -463,10 +466,10 @@
             t = same_side(k)
             line_send(t, pair_sum(t), r3.at[k - 1], rs3_r.at[0], t)
 
-    def line_gate():
+    def line_gate(steps):
         @pl.when(jnp.logical_not(outer))
         def _():
-            for i in range(far):
+            for i in steps:
                 t = from_far(i)
                 arrive(rg.at[i, pl.ds(0, near_side - 1)], rsg_r.at[0, i])
                 values = [part[0, cell(t, j)] for j in range(2)]
@@ -489,7 +492,7 @@
 
     def side_out(steps):
         for i in steps:
-            t = far_peer(i) if i < hi - 1 else top
+            t = low_peer(i) if i < hi - 1 else top
             arrive(r1.at[1, t, 0], rs1_r.at[1, t])
             s2[1, t] = (part[1, cell(t, 0)] + r1[1, t, 0].astype(jnp.float32)).astype(
                 jnp.bfloat16
@@ -508,32 +511,17 @@
         s4[t] = value.astype(jnp.bfloat16)
         push(s4.at[t], dst, 2, recv, owner(target, mid, core))
 
-    def side_line():
-        arrive(fbuf.at[0, pl.ds(0, hi * units)], rs1_r.at[1, hi])
-        for i in range(far):
-            t = from_far(i)
-            value = total(t)
-
-            @pl.when(outer)
-            def _():
-                send_last(t, value, rh.at[i, gate_slot], rsg_r.at[1, i], gate)
-
-            @pl.when(jnp.logical_not(outer))
-            def _():
-                arrive(rh.at[i, pl.ds(0, near_side - 1)], rsg_r.at[1, i])
-                merged = value
-                for k in range(near_side - 1):
-                    merged = merged + rh[i, k].astype(jnp.float32)
-                send_last(t, merged, r4.at[near_side - 1], rs3_r.at[1], t)
-
-        for k in range(1, near_side):
-            t = same_side(k)
-            send_last(t, total(t), r4.at[k - 1], rs3_r.at[1], t)
+    def side_line(steps):
+        if 0 in steps:
+            arrive(fbuf.at[0, pl.ds(0, hi * units)], rs1_r.at[1, hi])
+        for i in steps:
+            t = low_peer(i)
+            send_last(t, total(t), r4.at[top - at_least(top, t + 1)], rs3_r.at[1], t)
 
     def side_store():
         value = total(top)
         arrive(r4, rs3_r.at[1])
-        for k in range(near_side):
+        for k in range(hi - 1):
             value = value + r4[k].astype(jnp.float32)
         own1[...] = value * grad_scale
 
@@ -600,22 +588,25 @@
     for x in range(xs):
         for y, value in enumerate(layer_back(0, x)):
             keep_grad(1, x, y, value * slope[x, y])
+    halo_one = grad_halo(1)
+    line_gate((0,))
     late_relay()
     halo_wait(halo_in)
     turn_input(0, ahalo[0])
     turn_input(xs + 1, ahalo[1])
     terms_out(1)
-    line_gate()
+    line_gate(range(1, far))
     side_out(range(hi))
-    halo_one = grad_halo(1)
     late_follow()
-    side_line()
-    line_end()
+    side_line(range(1))
     halo_wait(halo_one)
     gather_core(1)
     for x in range(xs):
         for y, value in enumerate(layer_back(1, x)):
             gin[x, y] = value.astype(jnp.bfloat16)
+    side_line(range(1, hi - 2))
+    line_end()
+    side_line(range(hi - 2, hi - 1))
     line_store()
     side_store()
 
@@ -701,11 +692,10 @@
             pltpu.VMEM((hi // 2, 2) + piece, bf),
             pltpu.VMEM((hi // 2, hi // 2, 2) + piece, bf),
             pltpu.VMEM((hi,) + piece, bf),
-            pltpu.VMEM((hi // 2,) + piece, bf),
-            pltpu.VMEM((hi // 2, hi // 2) + piece, bf),
+            pltpu.VMEM((hi - 1,) + piece, bf),
             dma((6,)), dma((2,)), dma((3, 2)), dma((6,)),
             dma((hi,)), dma((hi,)), dma((2 * hi,)), dma((2,)), dma((4,)),
-            dma((2, hi + 1)), dma((2, hi)), dma((2,)), dma((2, hi // 2)),
+            dma((2, hi + 1)), dma((2, hi)), dma((2,)), dma((1, hi // 2)),
         ],
         compiler_params=pltpu.CompilerParams(collective_id=0, has_side_effects=True),
     )(

time: 35.7 us -> 34.1 us (0.955)
  the two profiles are of different devices: /device:TPU:0 before, /device:TPU:14 now
where the time goes in v4:
time: 34.1 us; the launch traced here: 34 us
  Pallas kernels  33.3 us (98%)
  between operations  0.64 us (2%)
    pallas_call x1, Pallas kernels, fused(): pl.pallas_call(functools.partial(kernel, n), out_shape=(pltpu.VMEM(grad_o...  32.5 us
    pallas_call x1, Pallas kernels, store_out(): pl.pallas_call(store_kernel, out_shape=tuple((jax.ShapeDtypeStruct(r.shap...  0.8 us

profile of v4, /device:TPU:14, one launch (start us, length us, event | category | flops | bytes accessed | tf_op | source)
XLA Modules:
  0.0 34.0 jit_solution(16272614906803895788)
XLA Ops:
  0.6 32.5 %shard_map.85 = (bf16[2,4,128,128]{3,2,1,0:T(8,128)(2,1)S(1)}, f32[27,8,128]{2,1,0:T(8,128)S(1)}, f32[27,8,128]{2,1,0:T(8,128)S(1)}) custom-call(bf16[2,4,128,128]{3,2,1,0:T(8,128)(2,1)} %go_in.1, bf16[2,4,128,128]{3,2,1,0:T(8,128)(2,1)} %xin_in.1, bf16[2,4,128,128]{3,2,1,0:T(8,128)(2,1)} %p1_in.1, bf16[2,4,128,128]{3,2,1,0:T(8,128)(2,1)} %p2_in.1, ...), custom_call_target="tpu_custom_call" | custom-call | tf_op jit(solution)/shard_map/pallas_call | solution.py:666
  33.2 0.8 %shard_map.86 = (bf16[2,4,128,128]{3,2,1,0:T(8,128)(2,1)}, f32[27,8,128]{2,1,0:T(8,128)}, f32[27,8,128]{2,1,0:T(8,128)}) custom-call(bf16[2,4,128,128]{3,2,1,0:T(8,128)(2,1)S(1)} %get-tuple-element.9.refs_0_, f32[27,8,128]{2,1,0:T(8,128)S(1)} %get-tuple-element.10.refs_1_, f32[27,8,128]{2,1,0:T(8,128)S(1)} %get-tuple-element.11.refs_2_), custom_call_target="tpu_custom_call" | custom-call | tf_op jit(solution)/shard_map/pallas_call | solution.py:647

commit v5 on v4

--- a/solution.py
+++ b/solution.py
@@ -165,8 +165,13 @@
     def same_side(k):
         return upper * far + (top - upper * far + k) % near_side
 
+    def ranked(j):
+        return (at_least(j, 1) - at_least(j, 2)) * (hi - 1) + at_least(j, 2) * (j - 1)
+
+    rank = at_least(top, 1) * (top + 1) - at_least(top, hi - 1) * (hi - 1)
+
     def low_peer(i):
-        return i + at_least(i + 1, top + 1)
+        return ranked(i + at_least(i + 1, rank + 1))
 
     def remote(src, dst, send, recv, target, plane):
         return pltpu.make_async_remote_copy(
@@ -418,8 +423,7 @@
     def side_of(j):
         return mid if j else 1 - mid
 
-    def scatter_core(s, i):
-        t = i if s else from_far(i)
+    def scatter_core(s, t):
         for j in range(2):
             s1[s, t, j] = part[s, chunk(t, side_of(j), 1 - core)].astype(jnp.bfloat16)
             if s:
@@ -427,14 +431,21 @@
         if not s:
             push(s1.at[s, t], r1.at[s, t], 1 + s, rs1_r.at[s, t], partner)
 
-    def terms_out(s, steps=range(3)):
-        for j in steps:
-            if s:
-                filter_terms_dense(s, j)
-            else:
-                filter_terms(s, (1 - upper) * (2 - j) + upper * j)
+    def terms_far():
+        for j in range(3):
+            filter_terms(0, (1 - upper) * (2 - j) + upper * j)
             for i in range(j * hi // 3, (j + 1) * hi // 3):
-                scatter_core(s, i)
+                scatter_core(0, from_far(i))
+
+    def terms_ranked():
+        ready, left_over = [], [0, hi - 1, *range(1, hi - 1)]
+        for a in (0, 2, 1):
+            filter_terms_dense(1, a)
+            ready.append(a)
+            for t in list(left_over):
+                if all(block in ready for block in range(3 * t // hi, -(-3 * (t + 1) // hi))):
+                    left_over.remove(t)
+                    scatter_core(1, t)
 
     def cell(t, j):
         return chunk(t, side_of(j), core)
@@ -573,12 +584,12 @@
         turn_input(x + 1, xin[x])
     loads[5].wait()
     first_line()
-    late_own()
-    late_spread()
     first_side()
     halo_wait(halo_two)
     halo_shifts(0)
-    terms_out(0)
+    late_own()
+    late_spread()
+    terms_far()
     first_relay()
     halo_in = saved_halo(2, xin)
     line_out()
@@ -594,7 +605,7 @@
     halo_wait(halo_in)
     turn_input(0, ahalo[0])
     turn_input(xs + 1, ahalo[1])
-    terms_out(1)
+    terms_ranked()
     line_gate(range(1, far))
     side_out(range(hi))
     late_follow()

time: 34.1 us -> 34.1 us (level)
  the two profiles are of different devices: /device:TPU:14 before, /device:TPU:0 now
where the time goes in v5:
time: 34.1 us; the launch traced here: 33.4 us
  Pallas kernels  32.8 us (96%)
  between operations  0.64 us (2%)
    pallas_call x1, Pallas kernels, fused(): pl.pallas_call(functools.partial(kernel, n), out_shape=(pltpu.VMEM(grad_o...  32 us
    pallas_call x1, Pallas kernels, store_out(): pl.pallas_call(store_kernel, out_shape=tuple((jax.ShapeDtypeStruct(r.shap...  0.8 us

profile of v5, /device:TPU:0, one launch (start us, length us, event | category | flops | bytes accessed | tf_op | source)
XLA Modules:
  0.0 33.4 jit_solution(8971939210680493604)
XLA Ops:
  0.6 32.0 %shard_map.85 = (bf16[2,4,128,128]{3,2,1,0:T(8,128)(2,1)S(1)}, f32[27,8,128]{2,1,0:T(8,128)S(1)}, f32[27,8,128]{2,1,0:T(8,128)S(1)}) custom-call(bf16[2,4,128,128]{3,2,1,0:T(8,128)(2,1)} %go_in.1, bf16[2,4,128,128]{3,2,1,0:T(8,128)(2,1)} %xin_in.1, bf16[2,4,128,128]{3,2,1,0:T(8,128)(2,1)} %p1_in.1, bf16[2,4,128,128]{3,2,1,0:T(8,128)(2,1)} %p2_in.1, ...), custom_call_target="tpu_custom_call" | custom-call | tf_op jit(solution)/shard_map/pallas_call | solution.py:677
  32.6 0.8 %shard_map.86 = (bf16[2,4,128,128]{3,2,1,0:T(8,128)(2,1)}, f32[27,8,128]{2,1,0:T(8,128)}, f32[27,8,128]{2,1,0:T(8,128)}) custom-call(bf16[2,4,128,128]{3,2,1,0:T(8,128)(2,1)S(1)} %get-tuple-element.9.refs_0_, f32[27,8,128]{2,1,0:T(8,128)S(1)} %get-tuple-element.10.refs_1_, f32[27,8,128]{2,1,0:T(8,128)S(1)} %get-tuple-element.11.refs_2_), custom_call_target="tpu_custom_call" | custom-call | tf_op jit(solution)/shard_map/pallas_call | solution.py:658
